TPU v7x, 128 devices: a whole 4x4x4 slice. The times are simulated.
128 devices in a mesh: elem: 8 (over y, core), bin: 16 (over z, x).
Axes of the slice: x: 4, y: 4, z: 4, core: 2. Of those that a mesh axis runs over, the one named last changes fastest.
Arguments:
- source: float32 [3, 128, 256, 128], P(None, 'elem', 'bin'), may hold values from -60 to 60
- viscosity: float32 [128, 256, 128], P('elem', 'bin'), may hold values from 0.3 to 3
- coarse_inverse: float32 [8, 128, 128], P('elem', 'bin'), may hold values from -0.06187184 to 2, as said below
- droplets: float32 [7, 8, 65536], P(None, 'elem', 'bin'), may hold values from -3 to 3, as said below
- droplet_elem: int32 [8, 65536], P('elem', 'bin'), may hold values from 0 to 63
- ghost_counts: int32 [2, 8, 16], P(None, 'elem', 'bin'), may hold values from 1 to 8, as said below
- tile_pairs: int32 [2, 8, 4096], P(None, 'elem', 'bin'), may hold values from 0 to 47, as said below
- tile_count: int32 [8, 16], P('elem', 'bin'), may hold values from 32 to 256, as said below
Outputs:
- velocity: float32 [3, 128, 256, 128], P(None, 'elem', 'bin')
- droplet_velocity: float32 [3, 8, 65536], P(None, 'elem', 'bin')
Inputs may be any that keep to these rules, and one draw needn't show every extreme that they name: `ghost_counts`: at least one bin sends 8 blocks to its lower neighbour and one to its upper neighbour. `tile_pairs`: row 0 names own blocks, below 32; row 1 names candidate blocks. `tile_count`: some bin uses all 256 tile slots. `droplets`: positions x, z and y lie in 0 to 1, diameters in 0.5 to 1.5. `coarse_inverse`: diagonal entries lie in 1 to 2.
All inputs are finite; a program needn't handle non-finite values.
Results may differ from a plain program's by a relative error of at most 0.0003.
Values sent between devices are 32-bit elements; how exact they have to be, the bound alone decides.
A program may use at most 128 MiB of HBM per device.

v0:
```python
import jax
import jax.numpy as jnp
import numpy as np
from jax import lax
from jax.sharding import PartitionSpec as P

ITERS = 4
NB = 32
BLOCK = 128
GMAX = 8
TGROUP = 16


PRECISE = lax.Precision.HIGHEST
MASS_TERM = 1.0
RELAXATION = 0.6
COARSE_GAIN = 0.02
SPREAD = 0.1
STIFFNESS = 0.3
TIME_STEP = 0.1


def extended(block, sides, width):
    for axis, dim in sides:
        count = lax.axis_size(axis)
        forward = [(i, i + 1) for i in range(count - 1)]
        forward.append((count - 1, 0))
        backward = [(target, source) for source, target in forward]
        low = lax.ppermute(
            lax.slice_in_dim(block, block.shape[dim] - width, None, axis=dim), axis, forward
        )
        high = lax.ppermute(lax.slice_in_dim(block, 0, width, axis=dim), axis, backward)
        block = jnp.concatenate([low, block, high], axis=dim)
    return block


def legendre_top(points):
    previous = points * 0.0 + 1.0
    current = points * 1.0
    for degree_index in range(1, 7):
        following = ((2 * degree_index + 1) * points * current - degree_index * previous) / (
            degree_index + 1
        )
        previous = current
        current = following
    return current


def gll_tables():
    points = np.array(
        [
            -1.0,
            -0.8717401485096066,
            -0.5917001814331423,
            -0.2092992179024789,
            0.2092992179024789,
            0.5917001814331423,
            0.8717401485096066,
            1.0,
        ]
    )
    weights = np.array(
        [
            0.03571428571428571,
            0.2107042271435061,
            0.3411226924835044,
            0.4124587946587038,
            0.4124587946587038,
            0.3411226924835044,
            0.2107042271435061,
            0.03571428571428571,
        ]
    )
    legendre = legendre_top(points)
    derivative = np.zeros((8, 8))
    for row_index in range(8):
        for col_index in range(8):
            if row_index != col_index:
                derivative[row_index, col_index] = (
                    legendre[row_index]
                    / legendre[col_index]
                    / (points[row_index] - points[col_index])
                )
    derivative[0, 0] = -14.0
    derivative[7, 7] = 14.0
    return (derivative.astype(np.float32), weights.astype(np.float32))


def seam_counts():
    return np.array([2.0, 1.0, 1.0, 1.0, 1.0, 1.0, 1.0, 2.0], np.float32)


def node_line(values, length):
    return jnp.asarray(np.tile(values, length // 8))


def nodal(line_x, line_y, line_z):
    return line_x[:, None, None] * line_y[None, :, None] * line_z[None, None, :]


def along(values, direction, matrix):
    amount = values.shape[direction] // 8
    divided = values.reshape(values.shape[:direction] + (amount, 8) + values.shape[direction + 1 :])
    contracted = jnp.tensordot(divided, matrix, axes=((direction + 1,), (1,)), precision=PRECISE)
    return jnp.moveaxis(contracted, -1, direction + 1).reshape(values.shape)


def seam_pass(values, direction, lower_plane, upper_plane):
    amount = values.shape[direction] // 8
    divided = values.reshape(values.shape[:direction] + (amount, 8) + values.shape[direction + 1 :])
    first_nodes = lax.index_in_dim(divided, 0, direction + 1, keepdims=False)
    last_nodes = lax.index_in_dim(divided, 7, direction + 1, keepdims=False)
    upper_sum = last_nodes + jnp.concatenate(
        [lax.slice_in_dim(first_nodes, 1, amount, axis=direction), upper_plane], direction
    )
    lower_sum = (
        jnp.concatenate(
            [lower_plane, lax.slice_in_dim(last_nodes, 0, amount - 1, axis=direction)], direction
        )
        + first_nodes
    )
    inner = lax.slice_in_dim(divided, 1, 7, axis=direction + 1)
    joined = jnp.concatenate(
        [
            jnp.expand_dims(lower_sum, direction + 1),
            inner,
            jnp.expand_dims(upper_sum, direction + 1),
        ],
        direction + 1,
    )
    return joined.reshape(values.shape)


def assemble(values):
    widened = extended(values, (("elem", 1), ("bin", 2)), 1)
    along_first = seam_pass(widened[:, 1:-1], 1, widened[:, :1], widened[:, -1:])
    along_second = seam_pass(
        along_first[:, :, 1:-1], 2, along_first[:, :, :1], along_first[:, :, -1:]
    )
    return seam_pass(along_second, 3, along_second[:, :, :, -1:], along_second[:, :, :, :1])


def prolong(coarse_cells):
    extent = coarse_cells.shape
    spread_cells = jnp.broadcast_to(
        coarse_cells[:, :, None, :, None, :, None],
        (extent[0], extent[1], 16, extent[2], 16, extent[3], 16),
    )
    return spread_cells.reshape(extent[0], extent[1] * 16, extent[2] * 16, extent[3] * 16)


def tile_force(candidates, own_block, cand_block, active):
    near_rows = candidates[own_block]
    far_rows = candidates[cand_block]
    distance = jnp.zeros((near_rows.shape[0], near_rows.shape[2], far_rows.shape[2]), jnp.float32)
    for component in range(3):
        offset = near_rows[:, component, :, None] - far_rows[:, component, None, :]
        distance = distance + offset * offset
    kernel = jnp.exp(-distance / SPREAD) * far_rows[:, 3, None, :] * active[:, None, None]
    summed = jnp.sum(kernel, axis=2)
    pulled = jnp.einsum("tab,tcb->tca", kernel, far_rows[:, :3], precision=PRECISE)
    return STIFFNESS * near_rows[:, 3, None, :] * (near_rows[:, :3] * summed[:, None, :] - pulled)


def collide_padded(candidates, tile_ids, limit):
    groups = tile_ids.shape[1] // TGROUP
    own_blocks = tile_ids[0].reshape(groups, TGROUP)
    cand_blocks = tile_ids[1].reshape(groups, TGROUP)
    positions = jnp.arange(groups * TGROUP, dtype=jnp.int32).reshape(groups, TGROUP)

    def advance(collision, entries):
        own_block, cand_block, position = entries
        active = (position < limit).astype(jnp.float32)
        return (
            collision.at[own_block].add(tile_force(candidates, own_block, cand_block, active)),
            None,
        )

    start_value = jnp.zeros((NB, 3, candidates.shape[2]), jnp.float32)
    collision, unused = lax.scan(advance, start_value, (own_blocks, cand_blocks, positions))
    return collision


def mask_size(part, kept):
    return jnp.concatenate([part[:3], part[3:] * kept[None, :]], 0)


def shift_height(part, amount):
    return jnp.concatenate([part[:1], part[1:2] + amount, part[2:]], 0)


def body(
    source, viscosity, coarse_inverse, droplets, droplet_elem, ghost_counts, tile_pairs, tile_count
):
    derivative, weights = gll_tables()
    deriv_table = jnp.asarray(derivative)
    square_table = deriv_table * deriv_table
    components, width_x, width_y, width_z = source.shape
    weight = nodal(
        node_line(weights, width_x), node_line(weights, width_y), node_line(weights, width_z)
    )
    multiplicity = nodal(
        node_line(seam_counts(), width_x),
        node_line(seam_counts(), width_y),
        node_line(seam_counts(), width_z),
    )
    coef_w = viscosity * weight
    identity = np.eye(width_z // 8, dtype=np.float32)
    forward_z = jnp.asarray(np.kron(identity, derivative.T))
    backward_z = jnp.asarray(np.kron(identity, derivative))
    square_z = jnp.asarray(np.kron(identity, derivative * derivative))

    def apply_local(component_field):
        summed = MASS_TERM * weight * component_field
        for direction in range(2):
            gradient = along(component_field, direction, deriv_table)
            summed = summed + along(coef_w * gradient, direction, deriv_table.T)
        gradient = jnp.dot(component_field, forward_z, precision=PRECISE)
        return summed + jnp.dot(coef_w * gradient, backward_z, precision=PRECISE)

    diagonal_local = MASS_TERM * weight
    for direction in range(2):
        diagonal_local = diagonal_local + along(coef_w, direction, square_table.T)
    diagonal_local = diagonal_local + jnp.dot(coef_w, square_z, precision=PRECISE)
    diag_sum = assemble(diagonal_local[None])[0]
    forcing = weight * source
    velocity = jnp.zeros_like(source)
    half_x, half_y, half_z = (width_x // 16, width_y // 16, width_z // 16)
    inverse_rows = coarse_inverse[0]
    for sweep_index in range(ITERS):
        if sweep_index == 0:
            residual = assemble(forcing)
        else:
            residual = assemble(
                forcing
                - jnp.stack([apply_local(velocity[component]) for component in range(components)])
            )
        coarse = (
            (weight * residual / multiplicity)
            .reshape(components, half_x, 16, half_y, 16, half_z, 16)
            .sum(axis=(2, 4, 6))
        )
        coarse = coarse.reshape(components, half_x * half_y * half_z)
        partial_dual = jnp.einsum("gh,cg->ch", inverse_rows, coarse, precision=PRECISE)
        coarse_dual = lax.psum(partial_dual, "bin")
        correction = jnp.einsum("gh,ch->cg", inverse_rows, coarse_dual, precision=PRECISE)
        correction = correction.reshape(components, half_x, half_y, half_z)
        velocity = velocity + assemble(
            (RELAXATION * residual / diag_sum + COARSE_GAIN * prolong(correction)) / multiplicity
        )
    element_mean = (weight * velocity).reshape(
        components, width_x // 8, 8, width_y // 8, 8, width_z // 8, 8
    ).sum(axis=(2, 4, 6)) / 8.0
    element_mean = element_mean.reshape(components, -1)
    own_drops = droplets[:, 0]
    position = jnp.stack([own_drops[0], own_drops[1], own_drops[2], own_drops[6]])
    span = GMAX * BLOCK
    block_ids = jnp.arange(span, dtype=jnp.int32) // BLOCK
    lower_count = ghost_counts[0, 0, 0]
    upper_count = ghost_counts[1, 0, 0]
    send_lower = mask_size(position[:, :span], (block_ids < lower_count).astype(jnp.float32))
    send_upper = mask_size(
        position[:, -span:], (block_ids >= GMAX - upper_count).astype(jnp.float32)
    )
    packet = jnp.concatenate([send_lower, send_upper], 1)
    widened = extended(packet, (("bin", 1),), span)
    from_below = shift_height(widened[:, :span], -1.0)
    from_above = shift_height(widened[:, -span:], 1.0)
    candidates = (
        jnp.concatenate([position, from_below, from_above], 1)
        .reshape(4, NB + 2 * GMAX, BLOCK)
        .transpose(1, 0, 2)
    )
    tile_ids = tile_pairs[:, 0]
    limit = tile_count[0, 0]
    collision = collide_padded(candidates, tile_ids, limit)
    collision = collision.transpose(1, 0, 2).reshape(3, own_drops.shape[1])
    element_ids = jnp.arange(element_mean.shape[1], dtype=jnp.int32)
    onehot = (droplet_elem[0][:, None] == element_ids[None, :]).astype(jnp.float32)
    sampled = jnp.einsum("ce,re->cr", element_mean, onehot, precision=PRECISE)
    speeds = own_drops[3:6]
    diameter = own_drops[6]
    updated = speeds + TIME_STEP * ((sampled - speeds) / (diameter * diameter) + collision)
    return (velocity, updated[:, None, :])


def solution(mesh):
    in_specs = (
        P(None, "elem", "bin", None),
        P("elem", "bin", None),
        P("elem", "bin", None),
        P(None, "elem", "bin"),
        P("elem", "bin"),
        P(None, "elem", "bin"),
        P(None, "elem", "bin"),
        P("elem", "bin"),
    )
    out_specs = (P(None, "elem", "bin", None), P(None, "elem", "bin"))
    return jax.shard_map(body, mesh=mesh, in_specs=in_specs, out_specs=out_specs, check_vma=False)
```

profile of v0, /device:TPU:0, one launch (start us, length us, event | category | flops | bytes accessed | tf_op | source)
XLA Modules:
  0.0 924.6 jit_solution(10439911834857078356)
XLA Ops:
  17.4 5.2 collective-permute-start.7
  39.1 5.9 collective-permute-start.3
  60.1 4.3 slice.1187
  74.6 5.9 fusion.32
  80.6 5.3 copy.1461
  86.2 37.4 %psum.28 = f32[3,128]{1,0:T(4,128)S(1)} all-reduce(f32[3,128]{1,0:T(4,128)S(1)} %fusion.112), channel_id=1, replica_groups=mesh['elem'=8,'bin'=16] {'bin'}, use_global_device_ids=true, to_apply=%region_2.0 | all-reduce | flops 384 | bytes 3072 | tf_op jit(solution)/shard_map/psum | solution.py:245
  139.1 5.2 collective-permute-start.11
  237.9 5.4 collective-permute-start.15
  253.7 4.3 slice.1259
  270.4 6.5 fusion.33
  276.9 5.2 copy.1544
  286.2 41.5 %psum.29 = f32[3,128]{1,0:T(4,128)} all-reduce(f32[3,128]{1,0:T(4,128)} %fusion.109), channel_id=1, replica_groups=mesh['elem'=8,'bin'=16] {'bin'}, use_global_device_ids=true, to_apply=%region_5.0 | all-reduce | flops 384 | bytes 3072 | tf_op jit(solution)/shard_map/psum | solution.py:245
  347.2 5.3 collective-permute-start.19
  364.6 4.2 slice.1282
  380.6 4.7 maximum_add_fusion
  451.0 5.3 collective-permute-start.23
  457.0 5.3 collective-permute-start.37
  469.6 4.3 slice.1308
  488.3 6.5 fusion.34
  494.8 5.2 copy.1610
  504.1 37.3 %psum.30 = f32[3,128]{1,0:T(4,128)} all-reduce(f32[3,128]{1,0:T(4,128)} %fusion.106), channel_id=1, replica_groups=mesh['elem'=8,'bin'=16] {'bin'}, use_global_device_ids=true, to_apply=%region_8.0 | all-reduce | flops 384 | bytes 3072 | tf_op jit(solution)/shard_map/psum | solution.py:245
  562.1 4.5 collective-permute-start.27
  580.6 4.2 slice.1331
  596.6 4.3 maximum_add_fusion.1
  666.8 5.3 collective-permute-start.31
  681.2 4.3 slice.1357
  696.0 6.0 fusion.35
  702.0 5.3 copy.1676
  707.5 40.4 %psum.31 = f32[3,128]{1,0:T(4,128)S(1)} all-reduce(f32[3,128]{1,0:T(4,128)S(1)} %fusion.103), channel_id=1, replica_groups=mesh['elem'=8,'bin'=16] {'bin'}, use_global_device_ids=true, to_apply=%region_11.12 | all-reduce | flops 384 | bytes 3072 | tf_op jit(solution)/shard_map/psum | solution.py:245
  759.3 5.3 collective-permute-start.35
  764.6 133.8 %while.10 = (s32[]{:T(128)}, f32[32,3,128]{2,1,0:T(4,128)S(1)}, s32[16,16]{1,0:T(8,128)}, f32[48,4,128]{2,1,0:T(4,128)S(1)}, s32[16,16]{1,0:T(8,128)}, /*index=5*/s32[16,16]{1,0:T(8,128)}, s32[]{:T(128)}, s32[]{:T(128)}) while((s32[]{:T(128)}, f32[32,3,128]{2,1,0:T(4,128)S(1)}, s32[16,16]{1,0:T(8,128)}, f32[48,4,128]{2,1,0:T(4,128)S(1)}, ...), condition=%wide.region_17.18_spmd, body=%wide.region_14.17_spmd.sunk | while | flops 16017570 | bytes 566241 | solution.py:180
  912.4 6.3 multiply_reduce_fusion
  (846 shorter events, 622.6 us)
Async XLA Ops:
  5.6 10.2 %collective-permute-start.4 = (f32[1,1,16,128]{3,2,1,0:T(8,128)S(1)}, f32[1,1,16,128]{3,2,1,0:T(8,128)S(1)}, u32[]{:S(2)}, u32[]{:S(2)}) collective-permute-start(f32[1,1,16,128]{3,2,1,0:T(8,128)S(1)} %get-tuple-element.284), channel_id=1, source_target_pairs={{0,16},{16,32},{32,48},{48,64},{64,80},{80,96},{96,112},{112,0},{1... | collective-permute-start | bytes 24584 | tf_op jit(solution)/shard_map/ppermute | solution.py:29
  5.6 10.2 %collective-permute-start.5 = (f32[1,1,16,128]{3,2,1,0:T(8,128)S(1)}, f32[1,1,16,128]{3,2,1,0:T(8,128)S(1)}, u32[]{:S(2)}, u32[]{:S(2)}) collective-permute-start(f32[1,1,16,128]{3,2,1,0:T(8,128)S(1)} %get-tuple-element.285), channel_id=1, source_target_pairs={{16,0},{32,16},{48,32},{64,48},{80,64},{96,80},{112,96},{0,112},{1... | collective-permute-start | bytes 24584 | tf_op jit(solution)/shard_map/ppermute | solution.py:32
  10.2 27.7 %collective-permute-start = (f32[3,1,16,128]{3,2,1,0:T(8,128)}, f32[3,1,16,128]{3,2,1,0:T(8,128)}, u32[]{:S(2)}, u32[]{:S(2)}) collective-permute-start(f32[3,1,16,128]{3,2,1,0:T(8,128)} %get-tuple-element.259), channel_id=1, source_target_pairs={{0,16},{16,32},{32,48},{48,64},{64,80},{80,96},{96,112},{112,0},{1... | collective-permute-start | bytes 73736 | tf_op jit(solution)/shard_map/ppermute | solution.py:29
  10.2 27.7 %collective-permute-start.1 = (f32[3,1,16,128]{3,2,1,0:T(8,128)}, f32[3,1,16,128]{3,2,1,0:T(8,128)}, u32[]{:S(2)}, u32[]{:S(2)}) collective-permute-start(f32[3,1,16,128]{3,2,1,0:T(8,128)} %get-tuple-element.260), channel_id=1, source_target_pairs={{16,0},{32,16},{48,32},{64,48},{80,64},{96,80},{112,96},{0,112},{1... | collective-permute-start | bytes 73736 | tf_op jit(solution)/shard_map/ppermute | solution.py:32
  15.8 8.1 collective-permute-start.6
  17.4 6.6 collective-permute-start.7
  39.1 11.4 %collective-permute-start.2 = (f32[3,18,1,128]{3,2,1,0:T(1,128)S(1)}, f32[3,18,1,128]{3,2,1,0:T(1,128)S(1)}, u32[]{:S(2)}, u32[]{:S(2)}) collective-permute-start(f32[3,18,1,128]{3,2,1,0:T(1,128)S(1)} %get-tuple-element.213), channel_id=1, source_target_pairs={{0,1},{1,2},{2,3},{3,4},{4,5},{5,6},{6,7},{7,8},{8,9},{9,10},{10,1... | collective-permute-start | bytes 82952 | tf_op jit(solution)/shard_map/ppermute | solution.py:29
  39.1 11.3 %collective-permute-start.3 = (f32[3,18,1,128]{3,2,1,0:T(1,128)S(1)}, f32[3,18,1,128]{3,2,1,0:T(1,128)S(1)}, u32[]{:S(2)}, u32[]{:S(2)}) collective-permute-start(f32[3,18,1,128]{3,2,1,0:T(1,128)S(1)} %get-tuple-element.214), channel_id=1, source_target_pairs={{1,0},{2,1},{3,2},{4,3},{5,4},{6,5},{7,6},{8,7},{9,8},{10,9},{11,1... | collective-permute-start | bytes 82952 | tf_op jit(solution)/shard_map/ppermute | solution.py:32
  129.2 6.6 collective-permute-start.8
  129.2 7.6 collective-permute-start.9
  139.0 7.2 collective-permute-start.10
  139.1 7.1 collective-permute-start.11
  237.8 7.2 collective-permute-start.14
  237.9 7.2 collective-permute-start.15
  336.1 6.6 collective-permute-start.16
  336.1 8.3 collective-permute-start.17
  347.1 7.5 collective-permute-start.18
  347.2 7.4 collective-permute-start.19
  450.9 11.4 %collective-permute-start.22 = (f32[3,18,1,128]{3,2,1,0:T(1,128)S(1)}, f32[3,18,1,128]{3,2,1,0:T(1,128)S(1)}, u32[]{:S(2)}, u32[]{:S(2)}) collective-permute-start(f32[3,18,1,128]{3,2,1,0:T(1,128)S(1)} %get-tuple-element.201), channel_id=1, source_target_pairs={{0,1},{1,2},{2,3},{3,4},{4,5},{5,6},{6,7},{7,8},{8,9},{9,10},{10,1... | collective-permute-start | bytes 82952 | tf_op jit(solution)/shard_map/ppermute | solution.py:29
  451.0 11.3 %collective-permute-start.23 = (f32[3,18,1,128]{3,2,1,0:T(1,128)S(1)}, f32[3,18,1,128]{3,2,1,0:T(1,128)S(1)}, u32[]{:S(2)}, u32[]{:S(2)}) collective-permute-start(f32[3,18,1,128]{3,2,1,0:T(1,128)S(1)} %get-tuple-element.202), channel_id=1, source_target_pairs={{1,0},{2,1},{3,2},{4,3},{5,4},{6,5},{7,6},{8,7},{9,8},{10,9},{11,1... | collective-permute-start | bytes 82952 | tf_op jit(solution)/shard_map/ppermute | solution.py:32
  457.0 208.2 %collective-permute-start.36 = (f32[4,1024]{1,0:T(4,128)}, f32[4,1024]{1,0:T(4,128)}, u32[]{:S(2)}, u32[]{:S(2)}) collective-permute-start(f32[4,1024]{1,0:T(4,128)} %get-tuple-element.291), channel_id=1, source_target_pairs={{0,1},{1,2},{2,3},{3,4},{4,5},{5,6},{6,7},{7,8},{8,9},{9,10},{10,1... | collective-permute-start | bytes 49160 | tf_op jit(solution)/shard_map/ppermute | solution.py:29
  457.0 215.1 %collective-permute-start.37 = (f32[4,1024]{1,0:T(4,128)}, f32[4,1024]{1,0:T(4,128)}, u32[]{:S(2)}, u32[]{:S(2)}) collective-permute-start(f32[4,1024]{1,0:T(4,128)} %get-tuple-element.292), channel_id=1, source_target_pairs={{1,0},{2,1},{3,2},{4,3},{5,4},{6,5},{7,6},{8,7},{9,8},{10,9},{11,1... | collective-permute-start | bytes 49160 | tf_op jit(solution)/shard_map/ppermute | solution.py:32
  549.7 6.6 collective-permute-start.24
  549.7 8.3 collective-permute-start.25
  561.3 8.6 collective-permute-start.26
  562.1 7.8 collective-permute-start.27
  666.7 7.7 collective-permute-start.30
  666.8 7.6 collective-permute-start.31
  752.6 6.3 collective-permute-start.32
  752.7 6.4 collective-permute-start.33
  759.2 139.2 %collective-permute-start.34 = (f32[3,18,1,128]{3,2,1,0:T(1,128)S(1)}, f32[3,18,1,128]{3,2,1,0:T(1,128)S(1)}, u32[]{:S(2)}, u32[]{:S(2)}) collective-permute-start(f32[3,18,1,128]{3,2,1,0:T(1,128)S(1)} %get-tuple-element.193), channel_id=1, source_target_pairs={{0,1},{1,2},{2,3},{3,4},{4,5},{5,6},{6,7},{7,8},{8,9},{9,10},{10,1... | collective-permute-start | bytes 82952 | tf_op jit(solution)/shard_map/ppermute | solution.py:29
  759.3 139.2 %collective-permute-start.35 = (f32[3,18,1,128]{3,2,1,0:T(1,128)S(1)}, f32[3,18,1,128]{3,2,1,0:T(1,128)S(1)}, u32[]{:S(2)}, u32[]{:S(2)}) collective-permute-start(f32[3,18,1,128]{3,2,1,0:T(1,128)S(1)} %get-tuple-element.194), channel_id=1, source_target_pairs={{1,0},{2,1},{3,2},{4,3},{5,4},{6,5},{7,6},{8,7},{9,8},{10,9},{11,1... | collective-permute-start | bytes 82952 | tf_op jit(solution)/shard_map/ppermute | solution.py:32
  (55 other events, 478.7 us)
where the time goes:
time: 935 us; the launch traced here: 925 us
  local copies, waits for them, and re-layouts  342 us (37%)
  other arithmetic  209 us (22%)
  blocking collectives  157 us (17%)
  matrix products  120 us (13%)
  starting transfers between devices  82.7 us (9%)
    psum x4, blocking collectives, body(): coarse_dual = lax.psum(partial_dual, 'bin')  157 us
    ppermute x19, starting transfers between devices, extended(): lax.ppermute(lax.slice_in_dim(block, 0, width, axis=dim), axis, backward)  79.5 us
    dot_general x38, matrix products, along(): jnp.tensordot(divided, matrix, axes=((direction + 1,), (1,)), precision=P...  48.1 us
    dot_general x16, matrix products, tile_force(): jnp.einsum('tab,tcb->tca', kernel, far_rows[:, :3], precision=PRECISE)  41.6 us
    another operation x18, local copies, waits for them, and re-layouts, along(): values.reshape(values.shape[:direction] + (amount, 8) + values.shape[dire...  38.6 us
    slice x27, local copies, waits for them, and re-layouts, seam_pass(): inner = lax.slice_in_dim(divided, 1, 7, axis=direction + 1)  35.8 us
    concatenate x16, local copies, waits for them, and re-layouts, seam_pass(): jnp.concatenate([jnp.expand_dims(lower_sum, direction + 1), inner, jnp.ex...  33 us
    slice x10, other arithmetic, seam_pass(): last_nodes = lax.index_in_dim(divided, 7, direction + 1, keepdims=False)  29.1 us
  transfers between devices with their start and end apart: 38, of which 10 were waited for; matrix products, arithmetic and copies ran while one was open for 35% of the time, Pallas kernels for 0%

commit v1 on v0

v1 whole, which is shorter than its diff:
```python
import functools

import jax
import jax.numpy as jnp
import numpy as np
from jax import lax
from jax.experimental import pallas as pl
from jax.experimental.pallas import tpu as pltpu
from jax.sharding import PartitionSpec as P

ITERS = 4
NB = 32
GMAX = 8
NCAND = NB + 2 * GMAX
TMAX = 256
KF = 32
MESH = pl.DeviceIdType.MESH

RELAXATION = 0.6
COARSE_GAIN = 0.02
STIFFNESS = 0.3
TIME_STEP = 0.1
ALPHA = float(np.log2(np.e) / 0.1)

F32 = jnp.float32
BF16 = jnp.bfloat16


def legendre_top(points):
    previous = points * 0.0 + 1.0
    current = points * 1.0
    for degree in range(1, 7):
        following = ((2 * degree + 1) * points * current - degree * previous) / (degree + 1)
        previous = current
        current = following
    return current


def gll_tables():
    half = [-1.0, -0.8717401485096066, -0.5917001814331423, -0.2092992179024789]
    points = np.array(half + [-value for value in reversed(half)])
    half = [0.03571428571428571, 0.2107042271435061, 0.3411226924835044, 0.4124587946587038]
    weights = np.array(half + list(reversed(half)))
    legendre = legendre_top(points)
    derivative = np.zeros((8, 8))
    for row in range(8):
        for col in range(8):
            if row != col:
                derivative[row, col] = (
                    legendre[row] / legendre[col] / (points[row] - points[col])
                )
    derivative[0, 0] = -14.0
    derivative[7, 7] = 14.0
    return derivative.astype(np.float32), weights.astype(np.float32)


DERIV, WEIGHTS = gll_tables()
COUNTS = np.array([2.0, 1.0, 1.0, 1.0, 1.0, 1.0, 1.0, 2.0], np.float32)
SHARE = WEIGHTS / COUNTS


def roll_tables(matrix):
    out = np.zeros((8, 8, 128), np.float32)
    for k in range(8):
        for i in range(8):
            out[k, i, :] = matrix[i, (i - k) % 8]
    return out


def vector_tables():
    wz = np.tile(WEIGHTS, 16)
    sz = np.tile(SHARE, 16)
    planes = [(WEIGHTS[:, None] * wz[None, :])[None], (SHARE[:, None] * sz[None, :])[None]]
    square = DERIV * DERIV
    planes += [roll_tables(DERIV), roll_tables(DERIV.T), roll_tables(square.T)]
    return np.concatenate(planes, 0).astype(np.float32)


def lane_tables():
    out = []
    identity = np.eye(16, dtype=np.float32)
    for matrix in (DERIV.T, DERIV, DERIV * DERIV):
        full = np.kron(identity, matrix)
        high = full.astype(jnp.bfloat16)
        low = (full - high.astype(np.float32)).astype(jnp.bfloat16)
        zero = np.zeros_like(low)
        top = np.concatenate([high, low], 1)
        out.append(np.concatenate([top, np.concatenate([high, zero], 1)], 0))
    return np.stack(out)


def split2(x):
    high = x.astype(BF16)
    return high, (x - high.astype(F32)).astype(BF16)


def split3(x):
    high = x.astype(BF16)
    rest = x - high.astype(F32)
    middle = rest.astype(BF16)
    return high, middle, (rest - middle.astype(F32)).astype(BF16)


def split3_wide(x):
    return [part.astype(F32) for part in split3(x)]


def mm(a, b):
    return jnp.dot(a, b, preferred_element_type=F32)


def lane_product(x, table):
    high, low = split2(x)
    both = mm(jnp.concatenate([high, low], 1), table)
    return both[:, :128] + both[:, 128:]


def exact_product(x, ones):
    rows = x.shape[0]
    out = mm(jnp.concatenate(split3(x), 0), ones)
    return out[:rows] + out[rows : 2 * rows] + out[2 * rows : 3 * rows]


def iota(shape, dim):
    return lax.broadcasted_iota(jnp.int32, shape, dim)


def kernel(
    n_elem,
    n_bin,
    tp_s,
    cnt_s,
    gc_s,
    src,
    visc,
    xin,
    drops,
    elem,
    own_v,
    tab,
    ztab,
    vel,
    dvel,
    coef,
    dinv,
    q,
    r,
    ysend,
    esend,
    xrecv,
    yrecv,
    erecv,
    rcs,
    crecv,
    xsend,
    xgat,
    wmat,
    gsend,
    grecv,
    nearf,
    farf,
    pf,
    near,
    far,
    pb,
    raw,
    oh,
    samp,
    hsend,
    hrecv,
    csend,
    crsem,
    xssem,
    xrsem,
    gssem,
    grsem,
):
    e = lax.axis_index("elem")
    b = lax.axis_index("bin")
    em, ep = lax.rem(e + n_elem - 1, n_elem), lax.rem(e + 1, n_elem)
    bm, bp = lax.rem(b + n_bin - 1, n_bin), lax.rem(b + 1, n_bin)
    total = 3 * n_bin - 1

    def each_partner(act):
        for de, row in ((0, e), (1, ep), (-1, em)):

            def step(db, carry, row=row, de=de):
                act(de, row, lax.rem(b + db, n_bin))
                return carry

            lax.fori_loop(1 if de == 0 else 0, n_bin, step, 0)

    barrier = pltpu.get_barrier_semaphore()
    each_partner(
        lambda de, row, col: pl.semaphore_signal(
            barrier, inc=1, device_id=(row, col), device_id_type=MESH
        )
    )

    lane = iota((8, 128), 1)
    sub = iota((8, 128), 0)
    lane8 = lax.rem(lane, 8)
    first_lane, last_lane = lane8 == 0, lane8 == 7
    first_sub, last_sub = sub == 0, sub == 7
    wyz = tab[0]
    syz = tab[1]

    def seam_z(v):
        up = pltpu.roll(v, 127, 1)
        down = pltpu.roll(v, 1, 1)
        return v + jnp.where(last_lane, up, jnp.where(first_lane, down, 0.0))

    def seam_inner(c, planes):
        out = []
        for low, high in planes:
            low, high = seam_z(low), seam_z(high)
            new_low = low + jnp.where(last_sub, pltpu.roll(high, 7, 0), 0.0)
            new_high = high + jnp.where(first_sub, pltpu.roll(low, 1, 0), 0.0)
            out.append((new_low, new_high))
        return out

    def store_planes(c, get):
        held = None
        for x in range(16):
            low, high = seam_inner(c, [get(x)])[0]
            if x == 7:
                held = (low, high)
                continue
            if x == 8:
                low, high = held[0] + low, held[1] + high
                q[c, 7, 0:8, :] = low
                q[c, 7, 8:16, :] = high
            q[c, x, 0:8, :] = low
            q[c, x, 8:16, :] = high

    def contract_rows(v, base):
        out = tab[base] * v
        for k in range(1, 8):
            out = out + tab[base + k] * pltpu.roll(v, k, 0)
        return out

    for x in range(16):
        for half in range(2):
            rows = pl.ds(8 * half, 8)
            coef[x, rows, :] = visc[x, rows, :] * (wyz * float(WEIGHTS[x % 8]))

    diag_z = lane_product(coef[...].reshape(256, 128), ztab[2])
    r[3] = diag_z.reshape(16, 16, 128)

    def diag_at(x):
        out = []
        for half in range(2):
            rows = pl.ds(8 * half, 8)
            total_d = r[3, x, rows, :] + wyz * float(WEIGHTS[x % 8])
            total_d = total_d + contract_rows(coef[x, rows, :], 18)
            start = (x // 8) * 8
            for i in range(8):
                factor = float(DERIV[i, x % 8] * DERIV[i, x % 8])
                total_d = total_d + factor * coef[start + i, rows, :]
            out.append(total_d)
        return tuple(out)

    store_planes(3, diag_at)

    def force_comp(c, carry):
        store_planes(
            c,
            lambda x: tuple(
                src[c, x, pl.ds(8 * half, 8), :] * (wyz * float(WEIGHTS[x % 8]))
                for half in range(2)
            ),
        )
        return carry

    lax.fori_loop(0, 3, force_comp, 0)

    q2 = q.reshape(4 * 256, 128)
    r2 = r.reshape(4 * 256, 128)
    edges = ((0, 0), (0, 15), (15, 0), (15, 15))

    def halo_copies(k, comps):
        side = pl.ds(0, comps)
        flat = pl.ds(0, comps * 16)

        def remote(src_ref, dst_ref, index, row, col):
            return pltpu.make_async_remote_copy(
                src_ref=src_ref,
                dst_ref=dst_ref,
                send_sem=hsend.at[k, index],
                recv_sem=hrecv.at[k, index],
                device_id=(row, col),
                device_id_type=MESH,
            )

        copies = [
            remote(q.at[side, 0], xrecv.at[k, 1, side], 0, em, b),
            remote(q.at[side, 15], xrecv.at[k, 0, side], 1, ep, b),
            remote(ysend.at[k, 0, flat], yrecv.at[k, 1, flat], 2, e, bm),
            remote(ysend.at[k, 1, flat], yrecv.at[k, 0, flat], 3, e, bp),
        ]
        for index, (x, y) in enumerate(edges):
            row = em if x == 0 else ep
            col = bm if y == 0 else bp
            copies.append(
                remote(esend.at[k, index], erecv.at[k, 3 - index], 4 + index, row, col)
            )
        return copies

    def halo_start(k, comps):
        ysend[k, 0, 0 : comps * 16, :] = q2[pl.ds(0, comps * 16, stride=16), :]
        ysend[k, 1, 0 : comps * 16, :] = q2[pl.ds(15, comps * 16, stride=16), :]
        for index, (x, y) in enumerate(edges):
            for c in range(4):
                if c < comps:
                    esend[k, index, c : c + 1, :] = q[c, x, y : y + 1, :]
                else:
                    esend[k, index, c : c + 1, :] = jnp.zeros((1, 128), F32)
        copies = halo_copies(k, comps)
        for copy in copies:
            copy.start()
        return copies

    def halo_finish(k, comps, copies):
        for copy in copies:
            copy.wait_recv()
        for c in range(comps):
            r[c, 1:15] = q[c, 1:15]
            r[c, 0] = q[c, 0] + xrecv[k, 0, c]
            r[c, 15] = q[c, 15] + xrecv[k, 1, c]
        low = pl.ds(0, comps * 16, stride=16)
        high = pl.ds(15, comps * 16, stride=16)
        r2[low, :] = r2[low, :] + yrecv[k, 0, 0 : comps * 16, :]
        r2[high, :] = r2[high, :] + yrecv[k, 1, 0 : comps * 16, :]
        for index, (x, y) in enumerate(edges):
            for c in range(comps):
                r[c, x, y : y + 1, :] = r[c, x, y : y + 1, :] + erecv[k, index, c : c + 1, :]

    fields = (0, 1, 2, 6)
    keep_low = (sub < gc_s[0]).astype(F32)
    keep_high = (sub >= GMAX - gc_s[1]).astype(F32)
    for index, field in enumerate(fields):
        low = drops[field, 0:GMAX, :]
        high = drops[field, NB - GMAX : NB, :]
        if field == 6:
            low, high = low * keep_low, high * keep_high
        gsend[0, index] = low
        gsend[1, index] = high
    xsend[...] = xin[0]

    pl.semaphore_wait(barrier, total)

    halos = [None] * ITERS
    halos[0] = halo_start(0, 4)
    ghosts = []
    for side, col in ((0, bm), (1, bp)):
        copy = pltpu.make_async_remote_copy(
            src_ref=gsend.at[side],
            dst_ref=grecv.at[1 - side],
            send_sem=gssem.at[side],
            recv_sem=grsem.at[side],
            device_id=(e, col),
            device_id_type=MESH,
        )
        copy.start()
        ghosts.append(copy)

    def send_x(de, row, col):
        pltpu.make_async_remote_copy(
            src_ref=xsend,
            dst_ref=xgat.at[(1 - de) * n_bin + b],
            send_sem=xssem.at[0],
            recv_sem=xrsem.at[0],
            device_id=(row, col),
            device_id_type=MESH,
        ).start()

    each_partner(send_x)

    def features(shape_rows, x, y, z, s):
        pass

    def near_rows(start, x, y, z):
        count = x.shape[0]
        place = lambda k: pl.ds(start * KF + k, count, stride=KF)
        k = 0
        for value in (x, y, z):
            high, middle, low = split3_wide(value * (2.0 * ALPHA))
            for part in (high, high, high, middle, middle, low):
                nearf[place(k), :] = part
                k += 1
        for part in split3_wide((x * x + y * y + z * z) * (-ALPHA)):
            nearf[place(k), :] = part
            k += 1
        for k in range(k, KF):
            value = 1.0 if k < 24 else 0.0
            nearf[place(k), :] = jnp.full(x.shape, value, F32)

    def far_rows(start, x, y, z, s):
        count = x.shape[0]
        place = lambda k: pl.ds(start * KF + k, count, stride=KF)
        k = 0
        for value in (x, y, z):
            high, middle, low = split3_wide(value)
            for part in (high, middle, low, high, middle, high):
                farf[place(k), :] = part
                k += 1
        for k in range(k, k + 3):
            farf[place(k), :] = jnp.full(x.shape, 1.0, F32)
        k += 1
        for part in split3_wide((x * x + y * y + z * z) * (-ALPHA)):
            farf[place(k), :] = part
            k += 1
        for k in range(k, KF):
            farf[place(k), :] = jnp.full(x.shape, 0.0, F32)
        for index, value in enumerate((s, s * x, s * y, s * z)):
            for level, part in enumerate(split3_wide(value)):
                pf[pl.ds(start * 16 + level * 4 + index, count, stride=16), :] = part
        for index in range(12, 16):
            pf[pl.ds(start * 16 + index, count, stride=16), :] = jnp.full(x.shape, 0.0, F32)

    def far_finish(start, groups):
        def step(g, carry):
            rows = pl.multiple_of((start + g * 4) * KF, 128)
            turned = farf[pl.ds(rows, 128), :].T
            for u in range(4):
                far[start + g * 4 + u] = turned[:, u * KF : (u + 1) * KF].astype(BF16)
            rows = pl.multiple_of((start + g * 4) * 16, 64)
            part = pf[pl.ds(rows, 64), :].astype(BF16).reshape(4, 16, 128)
            pb[pl.ds(start + g * 4, 4), :, 0:128] = part
            pb[pl.ds(start + g * 4, 4), :, 128:256] = part
            return carry

        lax.fori_loop(0, groups, step, 0)

    xa, ya, za, sa = drops[0] - 0.5, drops[1] - 0.5, drops[2] - 0.5, drops[6]
    near_rows(0, xa, ya, za)
    near[...] = nearf[...].astype(BF16).reshape(NB, KF, 128)
    far_rows(0, xa, ya, za, sa)
    far_finish(0, NB // 4)

    def onehot(i, carry):
        row = jnp.broadcast_to(elem[pl.ds(i, 1), :], (64, 128))
        oh[i] = (row == iota((64, 128), 0)).astype(F32).astype(BF16)
        return carry

    lax.fori_loop(0, NB, onehot, 0)

    for copy in ghosts:
        copy.wait_recv()
    far_rows(NB, grecv[0, 0] - 0.5, grecv[0, 1] - 1.5, grecv[0, 2] - 0.5, grecv[0, 3])
    far_rows(
        NB + GMAX, grecv[1, 0] - 0.5, grecv[1, 1] + 0.5, grecv[1, 2] - 0.5, grecv[1, 3]
    )
    far_finish(NB, 2 * GMAX // 4)

    def tiles(first, count, unroll=8):
        def step(i, carry):
            for j in range(unroll):
                t = first + i * unroll + j
                own, cand = tp_s[0, t], tp_s[1, t]
                g = jnp.exp2(mm(far[cand], near[own]))
                high, low = split2(g)
                out = mm(pb[cand], jnp.concatenate([high, low], 0))
                raw[pl.ds(pl.multiple_of(t * 16, 16), 16), :] = out
            return carry

        lax.fori_loop(0, count // unroll, step, 0)

    def coarse_setup():
        pltpu.make_async_copy(
            xgat.at[pl.ds(0, total)], xgat.at[pl.ds(0, total)], xrsem.at[0]
        ).wait()
        xgat[n_bin + b] = xsend[...]
        g, z = iota((128, 128), 0), iota((128, 128), 1)
        bin_of, cell = g // 8, lax.rem(g, 8)
        z_cell, z_in = z // 16, lax.rem(z, 16)
        other = jnp.where(z_in == 0, lax.rem(z_cell + 7, 8), lax.rem(z_cell + 1, 8))
        at_face = jnp.logical_or(z_in == 0, z_in == 15)
        value = jnp.where(cell == z_cell, jnp.where(at_face, 0.5, 1.0), 0.0)
        value = value + jnp.where(jnp.logical_and(at_face, cell == other), 0.5, 0.0)
        pick = lambda which: jnp.where(bin_of == which, value, 0.0)
        here = pick(b)
        spread = jnp.concatenate(
            [0.5 * (here + pick(bm)), here, 0.5 * (here + pick(bp))], 1
        ).astype(BF16)

        def line(l, carry):
            x = xgat[pl.ds(l * n_bin, n_bin)].reshape(128, 128)
            high, low = split2(x)
            turn = lambda p, w: lax.dot_general(
                p, w, (((1,), (1,)), ((), ())), preferred_element_type=F32
            )
            gram = turn(high, high) + turn(high, low) + turn(low, high)
            a, c2 = split2(exact_product(gram, spread))
            wmat[l, :, 0:384] = a
            wmat[l, :, 384:768] = c2
            return carry

        lax.fori_loop(0, 3, line, 0)

    lane128 = iota((128, 128), 0)
    gather_mat = (iota((128, 128), 1) == b * 8 + lane128 // 16).astype(F32).astype(BF16)
    bin_mask = [(iota((8, 128), 1) // 8 == sub + 8 * h) for h in range(2)]

    def coarse_start(k):
        sums = jnp.zeros((8, 128), F32)
        for c in range(3):
            acc = None
            for x in range(16):
                term = (r[c, x, 0:8, :] + r[c, x, 8:16, :]) * float(SHARE[x % 8])
                acc = term if acc is None else acc + term
            line = jnp.sum(acc * syz, axis=0, keepdims=True)
            sums = sums + jnp.where(sub == c, jnp.broadcast_to(line, (8, 128)), 0.0)
        placed = exact_product(sums, gather_mat)
        row = placed[0:1]
        row = row + pltpu.roll(placed[1:2], 40, 1) + pltpu.roll(placed[2:3], 80, 1)
        rcs[k] = row

        def send(de, row_id, col):
            pltpu.make_async_remote_copy(
                src_ref=rcs.at[k],
                dst_ref=crecv.at[k, (1 - de) * n_bin + b],
                send_sem=csend.at[k],
                recv_sem=crsem.at[k],
                device_id=(row_id, col),
                device_id_type=MESH,
            ).start()

        each_partner(send)

    def coarse_finish(k):
        pltpu.make_async_copy(
            crecv.at[k, pl.ds(0, total)], crecv.at[k, pl.ds(0, total)], crsem.at[k]
        ).wait()
        crecv[k, n_bin + b] = rcs[k]
        rows = crecv[k].reshape(3 * n_bin, 128)
        spread = []
        for l in range(3):
            rc = jnp.zeros((8, 128), F32)
            for c in range(3):
                acc = None
                for h in range(2):
                    part = rows[l * 16 + 8 * h : l * 16 + 8 * h + 8]
                    if c:
                        part = pltpu.roll(part, 128 - 40 * c, 1)
                    part = jnp.where(bin_mask[h], part, 0.0)
                    acc = part if acc is None else acc + part
                line = jnp.sum(acc, axis=0, keepdims=True)
                rc = rc + jnp.where(sub == c, jnp.broadcast_to(line, (8, 128)), 0.0)
            out = mm(jnp.concatenate(split2(rc), 0), wmat[l])
            spread.append(out[0:8, 0:384] + out[8:16, 0:384] + out[0:8, 384:768])
        low, here, high = spread
        classes = (
            (0.5 * COARSE_GAIN) * (here + low),
            COARSE_GAIN * here,
            (0.5 * COARSE_GAIN) * (here + high),
        )
        for c in range(3):
            fill = []
            for value in classes:
                wide = lambda yc: jnp.broadcast_to(
                    value[c : c + 1, yc * 128 : (yc + 1) * 128], (8, 128)
                )
                middle = wide(1)
                fill.append(
                    (jnp.where(first_sub, wide(0), middle), jnp.where(last_sub, wide(2), middle))
                )
            for x in range(16):
                which = 0 if x == 0 else (2 if x == 15 else 1)
                for half in range(2):
                    rows8 = pl.ds(8 * half, 8)
                    step = dinv[x, rows8, :] * r[c, x, rows8, :] + fill[which][half]
                    if k:
                        step = step + vel[c, x, rows8, :]
                    vel[c, x, rows8, :] = step

    def operator(c, carry):
        v_all = vel[c].reshape(256, 128)
        grad = lane_product(v_all, ztab[0]) * coef[...].reshape(256, 128)
        r[c] = lane_product(grad, ztab[1]).reshape(16, 16, 128)
        for part in range(2):
            for half in range(2):
                rows = pl.ds(8 * half, 8)
                v = [vel[c, 8 * part + i, rows, :] for i in range(8)]
                cf = [coef[8 * part + i, rows, :] for i in range(8)]
                out = [r[c, 8 * part + i, rows, :] for i in range(8)]
                for i in range(8):
                    gx = float(DERIV[i, 0]) * v[0]
                    for k in range(1, 8):
                        if DERIV[i, k] != 0:
                            gx = gx + float(DERIV[i, k]) * v[k]
                    gx = gx * cf[i]
                    for k in range(8):
                        if DERIV[i, k] != 0:
                            out[k] = out[k] + float(DERIV[i, k]) * gx
                for i in range(8):
                    gy = contract_rows(v[i], 2) * cf[i]
                    total_q = out[i] + contract_rows(gy, 10)
                    lead = src[c, 8 * part + i, rows, :] - v[i]
                    r[c, 8 * part + i, rows, :] = (
                        lead * (wyz * float(WEIGHTS[i])) - total_q
                    )
        store_planes(
            c, lambda x: (r[c, x, 0:8, :], r[c, x, 8:16, :])
        )
        return carry

    share = TMAX // 8
    done = 0
    for k in range(ITERS):
        comps = 4 if k == 0 else 3
        if k:
            for copy in halos[k - 1]:
                copy.wait_send()
            lax.fori_loop(0, 3, operator, 0)
            halos[k] = halo_start(k, comps)
        tiles(done, share)
        done += share
        halo_finish(k, comps, halos[k])
        if k == 0:
            dinv[...] = RELAXATION / r[3]
        coarse_start(k)
        if k == 0:
            coarse_setup()
        tiles(done, share)
        done += share
        coarse_finish(k)

    means = jnp.zeros((8, 128), F32)
    for part in range(2):
        for half in range(2):
            rows = pl.ds(8 * half, 8)
            sums = jnp.zeros((8, 128), F32)
            for c in range(3):
                acc = None
                for i in range(8):
                    term = vel[c, 8 * part + i, rows, :] * float(WEIGHTS[i])
                    acc = term if acc is None else acc + term
                line = jnp.sum(acc * wyz, axis=0, keepdims=True)
                sums = sums + jnp.where(sub == c, jnp.broadcast_to(line, (8, 128)), 0.0)
            base = (part * 2 + half) * 16
            place = jnp.where(iota((128, 128), 1) == base + lane128 // 8, 0.125, 0.0)
            means = means + exact_product(sums, place.astype(BF16))
    parts = jnp.concatenate(split3(means[:, 0:64]), 0)

    def sample(i, carry):
        out = mm(parts, oh[i])
        samp[pl.ds(pl.multiple_of(i * 8, 8), 8), :] = out[0:8] + out[8:16] + out[16:24]
        return carry

    lax.fori_loop(0, NB, sample, 0)

    slot = iota((NB, TMAX), 1)
    hit = jnp.logical_and(
        jnp.broadcast_to(own_v[0:1, :], (NB, TMAX)) == iota((NB, TMAX), 0), slot < cnt_s[0]
    )
    hit = hit.astype(F32).astype(BF16)
    sums = []
    for c in range(4):
        value = raw[pl.ds(c, TMAX, stride=16), :]
        value = value + raw[pl.ds(4 + c, TMAX, stride=16), :]
        value = value + raw[pl.ds(8 + c, TMAX, stride=16), :]
        out = mm(hit, jnp.concatenate(split3(value), 1))
        sums.append(out[:, 0:128] + out[:, 128:256] + out[:, 256:384])
    size = drops[6]
    for c in range(3):
        position = drops[c] - 0.5
        force = STIFFNESS * size * (position * sums[0] - sums[1 + c])
        speed = drops[3 + c]
        sampled = samp[pl.ds(c, NB, stride=8), :]
        dvel[c] = speed + TIME_STEP * ((sampled - speed) / (size * size) + force)

    for copy in halos[ITERS - 1]:
        copy.wait_send()
    for copy in ghosts:
        copy.wait_send()
    pltpu.make_async_copy(
        xgat.at[pl.ds(0, total)], xgat.at[pl.ds(0, total)], xssem.at[0]
    ).wait()
    for k in range(ITERS):
        pltpu.make_async_copy(
            crecv.at[k, pl.ds(0, total)], crecv.at[k, pl.ds(0, total)], csend.at[k]
        ).wait()


def body(
    n_elem,
    n_bin,
    source,
    viscosity,
    coarse_inverse,
    droplets,
    droplet_elem,
    ghost_counts,
    tile_pairs,
    tile_count,
):
    tp = tile_pairs.reshape(2, TMAX)
    vmem = pl.BlockSpec(memory_space=pltpu.VMEM)
    smem = pl.BlockSpec(memory_space=pltpu.SMEM)
    dma = pltpu.SemaphoreType.DMA
    velocity, updated = pl.pallas_call(
        functools.partial(kernel, n_elem, n_bin),
        out_shape=(
            jax.ShapeDtypeStruct((3, 16, 16, 128), F32),
            jax.ShapeDtypeStruct((3, NB, 128), F32),
        ),
        in_specs=[smem] * 3 + [vmem] * 8,
        out_specs=(vmem, vmem),
        scratch_shapes=[
            pltpu.VMEM((16, 16, 128), F32),
            pltpu.VMEM((16, 16, 128), F32),
            pltpu.VMEM((4, 16, 16, 128), F32),
            pltpu.VMEM((4, 16, 16, 128), F32),
            pltpu.VMEM((ITERS, 2, 64, 128), F32),
            pltpu.VMEM((ITERS, 4, 4, 128), F32),
            pltpu.VMEM((ITERS, 2, 4, 16, 128), F32),
            pltpu.VMEM((ITERS, 2, 64, 128), F32),
            pltpu.VMEM((ITERS, 4, 4, 128), F32),
            pltpu.VMEM((ITERS, 1, 128), F32),
            pltpu.VMEM((ITERS, 3 * n_bin, 1, 128), F32),
            pltpu.VMEM((8, 128), F32),
            pltpu.VMEM((3 * n_bin, 8, 128), F32),
            pltpu.VMEM((3, 128, 768), BF16),
            pltpu.VMEM((2, 4, GMAX, 128), F32),
            pltpu.VMEM((2, 4, GMAX, 128), F32),
            pltpu.VMEM((NB * KF, 128), F32),
            pltpu.VMEM((NCAND * KF, 128), F32),
            pltpu.VMEM((NCAND * 16, 128), F32),
            pltpu.VMEM((NB, KF, 128), BF16),
            pltpu.VMEM((NCAND, 128, KF), BF16),
            pltpu.VMEM((NCAND, 16, 256), BF16),
            pltpu.VMEM((TMAX * 16, 128), F32),
            pltpu.VMEM((NB, 64, 128), BF16),
            pltpu.VMEM((NB * 8, 128), F32),
            dma((ITERS, 8)),
            dma((ITERS, 8)),
            dma((ITERS,)),
            dma((ITERS,)),
            dma((1,)),
            dma((1,)),
            dma((2,)),
            dma((2,)),
        ],
        compiler_params=pltpu.CompilerParams(
            collective_id=0, has_side_effects=True, vmem_limit_bytes=48 * 1024 * 1024
        ),
        name="sweeps",
    )(
        tp,
        tile_count.reshape(1),
        ghost_counts.reshape(2),
        source,
        viscosity,
        coarse_inverse,
        droplets.reshape(7, NB, 128),
        droplet_elem.reshape(NB, 128),
        tp,
        jnp.asarray(vector_tables()),
        jnp.asarray(lane_tables()),
    )
    return velocity, updated.reshape(3, 1, NB * 128)


def solution(mesh):
    in_specs = (
        P(None, "elem", "bin", None),
        P("elem", "bin", None),
        P("elem", "bin", None),
        P(None, "elem", "bin"),
        P("elem", "bin"),
        P(None, "elem", "bin"),
        P(None, "elem", "bin"),
        P("elem", "bin"),
    )
    out_specs = (P(None, "elem", "bin", None), P(None, "elem", "bin"))
    run = functools.partial(body, mesh.shape["elem"], mesh.shape["bin"])
    return jax.shard_map(run, mesh=mesh, in_specs=in_specs, out_specs=out_specs, check_vma=False)
```

time: 935 us -> 76.9 us (0.08)
  local copies, waits for them, and re-layouts: 342 us -> 8.09 us
  other arithmetic: 209 us -> 0 us
  blocking collectives: 157 us -> 0 us
  matrix products: 120 us -> 0 us
  starting transfers between devices: 82.7 us -> 0 us
  Pallas kernels: 0 us -> 66.4 us
    psum x4 -> x0, blocking collectives: 157 us -> none  [body(): coarse_dual = lax.psum(partial_dual, 'bin')]
    dot_general x82 -> x0, matrix products: 120 us -> none  [the longest x38 48.1 us: along(): jnp.tensordot(divided, matrix, axes=((direction + 1,), (1,)), precision=P...]
    slice x137 -> x0, local copies, waits for them, and re-layouts: 102 us -> none  [the longest x27 35.8 us: seam_pass(): inner = lax.slice_in_dim(divided, 1, 7, axis=direction + 1)]
    ppermute x38 -> x0, starting transfers between devices: 82.7 us -> none  [the longest x19 79.5 us: extended(): lax.ppermute(lax.slice_in_dim(block, 0, width, axis=dim), axis, backward)]
    pallas_call x0 -> x1, Pallas kernels: none -> 66.4 us  [body(): pl.pallas_call(functools.partial(kernel, n_elem, n_bin), out_shape=(jax.S...]
    concatenate x85 -> x0, local copies, waits for them, and re-layouts: 65.3 us -> none  [the longest x16 33 us: seam_pass(): jnp.concatenate([jnp.expand_dims(lower_sum, direction + 1), inner, jnp.ex...]
    reduce_sum x26 -> x0, other arithmetic: 55.3 us -> none  [the longest x8 27.9 us: body(): coarse = (weight * residual / multiplicity).reshape(components, half_x, 1...]
    another operation x20 -> x0, local copies, waits for them, and re-layouts: 41.3 us -> none  [the longest x18 38.6 us: along(): values.reshape(values.shape[:direction] + (amount, 8) + values.shape[dire...]
  transfers between devices with their start and end apart: 38 -> 0, of which waited for: 10 -> 0; matrix products, arithmetic and copies ran while one was open for 35% -> 0% of each run, Pallas kernels for 0% -> 0%
where the time goes in v1:
time: 76.9 us; the launch traced here: 75.8 us
  Pallas kernels  66.4 us (86%)
  local copies, waits for them, and re-layouts  8.09 us (11%)
  between operations  1.31 us (2%)
    pallas_call x1, Pallas kernels, body(): pl.pallas_call(functools.partial(kernel, n_elem, n_bin), out_shape=(jax.S...  66.4 us
    unnamed x21, local copies, waits for them, and re-layouts  8.09 us

profile of v1, /device:TPU:0, one launch (start us, length us, event | category | flops | bytes accessed | tf_op | source)
XLA Modules:
  0.0 75.8 jit_solution(2124740636753155116)
XLA Ops:
  1.3 0.0 copy-start.8
  1.3 0.0 copy-start.6
  1.3 0.7 copy-done.8
  2.0 0.0 copy-start.7
  2.0 0.0 copy-done.6
  2.0 0.6 copy-done.7
  2.6 0.0 copy-start
  2.6 1.0 %copy-done = f32[3,16,16,128]{3,2,1,0:T(8,128)S(1)} copy-done((f32[3,16,16,128]{3,2,1,0:T(8,128)S(1)}, f32[3,16,16,128]{3,2,1,0:T(8,128)}, u32[]{:S(2)}) %copy-start) | copy-done | bytes 393240
  3.6 0.0 copy-start.1
  3.6 1.0 %copy-done.1 = bf16[3,256,256]{2,1,0:T(8,128)(2,1)S(1)} copy-done((bf16[3,256,256]{2,1,0:T(8,128)(2,1)S(1)}, bf16[3,256,256]{2,1,0:T(8,128)(2,1)}, u32[]{:S(2)}) %copy-start.1) | copy-done | bytes 393240
  4.6 0.0 copy-start.2
  4.6 0.9 %copy-done.2 = f32[16,16,128]{2,1,0:T(8,128)S(1)} copy-done((f32[16,16,128]{2,1,0:T(8,128)S(1)}, f32[16,16,128]{2,1,0:T(8,128)}, u32[]{:S(2)}) %copy-start.2) | copy-done | bytes 131096
  5.5 0.0 copy-start.3
  5.5 0.9 %copy-done.3 = f32[7,1,4096]{2,1,0:T(1,128)S(1)} copy-done((f32[7,1,4096]{2,1,0:T(1,128)S(1)}, f32[7,1,4096]{2,1,0:T(1,128)}, u32[]{:S(2)}) %copy-start.3) | copy-done | bytes 114712
  6.4 0.0 copy-start.4
  6.4 0.9 %copy-done.4 = f32[26,8,128]{2,1,0:T(8,128)S(1)} copy-done((f32[26,8,128]{2,1,0:T(8,128)S(1)}, f32[26,8,128]{2,1,0:T(8,128)}, u32[]{:S(2)}) %copy-start.4) | copy-done | bytes 106520
  7.3 0.0 copy-start.5
  7.3 0.7 copy-done.5
  8.0 66.4 %sweeps.1 = (f32[3,16,16,128]{3,2,1,0:T(8,128)S(1)}, f32[3,32,128]{2,1,0:T(8,128)S(1)}) custom-call(s32[2,256]{1,0:T(2,128)S(1)} %bitcast.11, s32[1]{0:T(128)} %bitcast.8.cnt_s, s32[2]{0:T(128)S(1)} %bitcast.14, f32[3,16,16,128]{3,2,1,0:T(8,128)S(1)} %copy-done, f32[16,16,128]{2,1,0:T(8,128)S(1)} %copy-done.2, f32[1,8,128]{2,1,0:T(8,128)S(1)} %copy-done.6, ...), custom_call_target="tpu_custom_call" | custom-call | tf_op jit(solution)/shard_map/sweeps/pallas_call | solution.py:702
  74.4 0.7 copy.20
  75.2 0.6 copy.21
  (1 shorter events, 0.0 us)
Async XLA Ops:
  1.3 0.7 copy-start.8
  1.3 0.7 copy-start.6
  2.0 0.7 copy-start.7
  2.6 1.0 %copy-start = (f32[3,16,16,128]{3,2,1,0:T(8,128)S(1)}, f32[3,16,16,128]{3,2,1,0:T(8,128)}, u32[]{:S(2)}) copy-start(f32[3,16,16,128]{3,2,1,0:T(8,128)} %src.1) | copy-start | bytes 1179652
  3.6 1.0 %copy-start.1 = (bf16[3,256,256]{2,1,0:T(8,128)(2,1)S(1)}, bf16[3,256,256]{2,1,0:T(8,128)(2,1)}, u32[]{:S(2)}) copy-start(bf16[3,256,256]{2,1,0:T(8,128)(2,1)} %constant.5.clone.ztab) | copy-start | bytes 1179652
  4.6 0.9 %copy-start.2 = (f32[16,16,128]{2,1,0:T(8,128)S(1)}, f32[16,16,128]{2,1,0:T(8,128)}, u32[]{:S(2)}) copy-start(f32[16,16,128]{2,1,0:T(8,128)} %visc.1) | copy-start | bytes 393220
  5.5 0.9 %copy-start.3 = (f32[7,1,4096]{2,1,0:T(1,128)S(1)}, f32[7,1,4096]{2,1,0:T(1,128)}, u32[]{:S(2)}) copy-start(f32[7,1,4096]{2,1,0:T(1,128)} %param.13) | copy-start | bytes 344068
  6.4 0.9 %copy-start.4 = (f32[26,8,128]{2,1,0:T(8,128)S(1)}, f32[26,8,128]{2,1,0:T(8,128)}, u32[]{:S(2)}) copy-start(f32[26,8,128]{2,1,0:T(8,128)} %constant.4.clone.tab) | copy-start | bytes 319492
  7.3 0.7 copy-start.5
